TPU v7x, 32 devices: a whole 2x2x4 slice. The times are simulated.
32 devices in a mesh: ctx: 8 (over z, x), wt: 4 (over y, core).
Axes of the slice: x: 2, y: 2, z: 4, core: 2. Of those that a mesh axis runs over, the one named last changes fastest.
Arguments:
- hidden_in: bfloat16 [2, 4, 1024, 960], P(None, 'wt', 'ctx'), may hold values from -6 to 6
- d_out: bfloat16 [2, 4, 1024, 960], P(None, 'wt', 'ctx'), may hold values from -6 to 6
- block_order: int32 [2, 16], replicated, may hold values from 0 to 15, as said below
- gain_attn: bfloat16 [960], P('wt'), may hold values from 0.5 to 1.5
- gain_mlp: bfloat16 [960], P('wt'), may hold values from 0.5 to 1.5
- w_q: bfloat16 [960, 960], P('wt'), may hold values from -0.25 to 0.25
- w_kv: bfloat16 [960, 640], P('wt'), may hold values from -0.1875 to 0.1875
- w_o: bfloat16 [960, 960], P('wt'), may hold values from -3 to 3
- w_gu: bfloat16 [960, 5120], P('wt'), may hold values from -0.1875 to 0.1875
- w_down: bfloat16 [2560, 960], P('wt'), may hold values from -0.25 to 0.25
Outputs:
- hidden_out: bfloat16 [2, 4, 1024, 960], P(None, 'wt', 'ctx')
- grad_in: bfloat16 [2, 4, 1024, 960], P(None, 'wt', 'ctx')
- grad_gain_attn: float32 [960], P('wt')
- grad_gain_mlp: float32 [960], P('wt')
- grad_w_q: float32 [960, 960], P('wt')
- grad_w_kv: float32 [960, 640], P('wt')
- grad_w_o: float32 [960, 960], P('wt')
- grad_w_gu: float32 [960, 5120], P('wt')
- grad_w_down: float32 [2560, 960], P('wt')
Inputs may be any that keep to these rules, and one draw needn't show every extreme that they name: block_order[m] is a permutation of the 16 blocks in which stored blocks 2c and 2c + 1 are a mirrored pair: their numbers add up to 15.
All inputs are finite; a program needn't handle non-finite values.
Results may differ from a plain program's by a relative error of at most 0.018.
Values may be sent and summed in bfloat16 or wider, within the bound.
A program may use at most 256 MiB of HBM per device.

v0:
```python
import math
import jax
import jax.numpy as jnp
from jax import lax
from jax.sharding import PartitionSpec as P

QH = 15
KVH = 5
HD = 64
eps_norm = 1e-05
rope_base = 10000.0


def norm_scale(values, gain):
    return values * lax.rsqrt(jnp.mean(values * values, axis=-1, keepdims=True) + eps_norm) * gain


def rope_tables(positions):
    half_dim = HD // 2
    frequency = jnp.exp(jnp.arange(half_dim, dtype=jnp.float32) * (-2.0 * math.log(rope_base) / HD))
    angles = positions.astype(jnp.float32)[:, None] * frequency[None, :]
    return (jnp.cos(angles), jnp.sin(angles))


def rotate(values, cosine, sine):
    half_dim = values.shape[-1] // 2
    first_half = values[..., :half_dim]
    second_half = values[..., half_dim:]
    cos_wide = cosine[:, None, :]
    sin_wide = sine[:, None, :]
    return jnp.concatenate(
        [
            first_half * cos_wide - second_half * sin_wide,
            second_half * cos_wide + first_half * sin_wide,
        ],
        axis=-1,
    )


def unrotate(values, cosine, sine):
    half_dim = values.shape[-1] // 2
    first_half = values[..., :half_dim]
    second_half = values[..., half_dim:]
    cos_wide = cosine[:, None, :]
    sin_wide = sine[:, None, :]
    return jnp.concatenate(
        [
            first_half * cos_wide + second_half * sin_wide,
            second_half * cos_wide - first_half * sin_wide,
        ],
        axis=-1,
    )


def block_size(total_rows, limit):
    best_size = 1
    for candidate in range(1, min(total_rows, limit) + 1):
        if total_rows % candidate == 0:
            best_size = candidate
    return best_size


def outer_sum(left, right):
    return lax.dot_general(
        left, right, (((0,), (0,)), ((), ())), preferred_element_type=jnp.float32
    )


def back_product(left, weight):
    return lax.dot_general(
        left, weight, (((1,), (1,)), ((), ())), preferred_element_type=jnp.float32
    )


def block_scores(query_groups, keys_block, key_pos, row_pos, score_scale):
    scores = (
        jnp.einsum("hrd,khd->hrk", query_groups, keys_block, preferred_element_type=jnp.float32)
        * score_scale
    )
    visible = key_pos[None, None, :] <= row_pos[None, :, None]
    return (scores, visible)


def local(hidden_in, d_out, block_order, gain_attn, gain_mlp, w_q, w_kv, w_o, w_gu, w_down):
    gathered = (
        lax.all_gather(gain_attn, "wt", axis=0, tiled=True),
        lax.all_gather(gain_mlp, "wt", axis=0, tiled=True),
        lax.all_gather(w_q, "wt", axis=0, tiled=True),
        lax.all_gather(w_kv, "wt", axis=0, tiled=True),
        lax.all_gather(w_o, "wt", axis=0, tiled=True),
        lax.all_gather(w_gu, "wt", axis=0, tiled=True),
        lax.all_gather(w_down, "wt", axis=0, tiled=True),
    )
    gain_one = gathered[0].astype(jnp.float32)
    gain_two = gathered[1].astype(jnp.float32)
    weight_q, weight_kv, weight_o, weight_gu, weight_down = (
        gathered[2],
        gathered[3],
        gathered[4],
        gathered[5],
        gathered[6],
    )
    micro_count = hidden_in.shape[0]
    seg_rows = hidden_in.shape[2]
    n_ctx = lax.axis_size("ctx")
    seq_len = seg_rows * n_ctx
    half_block = seg_rows // 2
    kv_width = KVH * HD
    group_size = QH // KVH
    row_count = group_size * seg_rows
    ff_width = weight_down.shape[0]
    key_block = block_size(seq_len, 1024)
    block_count = seq_len // key_block
    score_scale = 1.0 / math.sqrt(HD)
    my_start = lax.axis_index("ctx") * seg_rows
    grad_names = [jnp.zeros(item.shape, jnp.float32) for item in gathered]
    outputs = []
    input_grads = []
    for micro_index in range(micro_count):
        tokens_in = hidden_in[micro_index, 0].astype(jnp.float32)
        order_row = block_order[micro_index]
        key_pos = (
            order_row[:, None] * half_block + jnp.arange(half_block, dtype=jnp.int32)[None, :]
        ).reshape(seq_len)
        query_pos = lax.dynamic_slice_in_dim(key_pos, my_start, seg_rows)
        row_pos = jnp.tile(query_pos, group_size)
        cosine, sine = rope_tables(query_pos)
        normed_one, pull_one = jax.vjp(norm_scale, tokens_in, gain_one)
        act_one = normed_one.astype(jnp.bfloat16)
        query_lin = jnp.dot(act_one, weight_q, preferred_element_type=jnp.float32).reshape(
            seg_rows, QH, HD
        )
        query_rot = rotate(query_lin, cosine, sine).astype(jnp.bfloat16)
        query_groups = (
            query_rot.reshape(seg_rows, KVH, group_size, HD)
            .transpose(1, 2, 0, 3)
            .reshape(KVH, row_count, HD)
        )
        kv_lin = jnp.dot(act_one, weight_kv, preferred_element_type=jnp.float32)
        key_rot = rotate(kv_lin[:, :kv_width].reshape(seg_rows, KVH, HD), cosine, sine).reshape(
            seg_rows, kv_width
        )
        kv_send = jnp.concatenate([key_rot, kv_lin[:, kv_width:]], axis=1).astype(jnp.bfloat16)
        kv_whole = lax.all_gather(kv_send, "ctx", axis=0, tiled=True)
        kv_blocks = kv_whole.reshape(block_count, key_block, 2 * kv_width)
        pos_blocks = key_pos.reshape(block_count, key_block)

        def lse_step(carry, item):
            top_now, total_now = carry
            kv_block, kpos = item
            keys_block = kv_block[:, :kv_width].reshape(key_block, KVH, HD)
            scores, visible = block_scores(query_groups, keys_block, kpos, row_pos, score_scale)
            top_new = jnp.maximum(top_now, jnp.max(jnp.where(visible, scores, -1e30), axis=-1))
            total_new = total_now * jnp.exp(top_now - top_new) + jnp.sum(
                jnp.where(visible, jnp.exp(scores - top_new[..., None]), 0.0), axis=-1
            )
            return ((top_new, total_new), None)

        start_top = jnp.full((KVH, row_count), -1e30, jnp.float32)
        start_total = jnp.zeros((KVH, row_count), jnp.float32)
        (top_all, total_all), _ = lax.scan(
            lse_step, (start_top, start_total), (kv_blocks, pos_blocks)
        )
        lse = top_all + jnp.log(total_all)

        def value_step(acc_now, item):
            kv_block, kpos = item
            keys_block = kv_block[:, :kv_width].reshape(key_block, KVH, HD)
            vals_block = kv_block[:, kv_width:].reshape(key_block, KVH, HD)
            scores, visible = block_scores(query_groups, keys_block, kpos, row_pos, score_scale)
            probs = jnp.where(visible, jnp.exp(scores - lse[..., None]), 0.0).astype(jnp.bfloat16)
            return (
                acc_now
                + jnp.einsum("hrk,khd->hrd", probs, vals_block, preferred_element_type=jnp.float32),
                None,
            )

        acc_all, _ = lax.scan(
            value_step, jnp.zeros((KVH, row_count, HD), jnp.float32), (kv_blocks, pos_blocks)
        )
        attn_low = (
            acc_all.reshape(KVH, group_size, seg_rows, HD)
            .transpose(2, 0, 1, 3)
            .reshape(seg_rows, QH * HD)
            .astype(jnp.bfloat16)
        )
        mid_state = tokens_in + jnp.dot(attn_low, weight_o, preferred_element_type=jnp.float32)
        normed_two, pull_two = jax.vjp(norm_scale, mid_state, gain_two)
        act_two = normed_two.astype(jnp.bfloat16)
        gate_up = jnp.dot(act_two, weight_gu, preferred_element_type=jnp.float32)
        gate_part = gate_up[:, :ff_width]
        up_part = gate_up[:, ff_width:]
        sig_gate = jax.nn.sigmoid(gate_part)
        hidden_low = (gate_part * sig_gate * up_part).astype(jnp.bfloat16)
        result = mid_state + jnp.dot(hidden_low, weight_down, preferred_element_type=jnp.float32)
        outputs.append(result.astype(jnp.bfloat16))
        grad_low = d_out[micro_index, 0]
        grad_top = grad_low.astype(jnp.float32)
        grad_down = outer_sum(hidden_low, grad_low)
        d_hidden = back_product(grad_low, weight_down)
        d_gate = d_hidden * up_part * sig_gate * (1.0 + gate_part * (1.0 - sig_gate))
        d_up = d_hidden * gate_part * sig_gate
        d_gu_low = jnp.concatenate([d_gate, d_up], axis=1).astype(jnp.bfloat16)
        grad_gu = outer_sum(act_two, d_gu_low)
        d_act_two = back_product(d_gu_low, weight_gu)
        d_mid_norm, grad_gain_two = pull_two(d_act_two)
        d_mid = grad_top + d_mid_norm
        d_mid_low = d_mid.astype(jnp.bfloat16)
        grad_o = outer_sum(attn_low, d_mid_low)
        d_attn_low = back_product(d_mid_low, weight_o).astype(jnp.bfloat16)
        grad_groups = (
            d_attn_low.reshape(seg_rows, KVH, group_size, HD)
            .transpose(1, 2, 0, 3)
            .reshape(KVH, row_count, HD)
        )
        kv_back = lax.all_gather(kv_send, "ctx", axis=0, tiled=True).reshape(
            block_count, key_block, 2 * kv_width
        )

        def delta_step(delta_now, item):
            kv_block, kpos = item
            keys_block = kv_block[:, :kv_width].reshape(key_block, KVH, HD)
            vals_block = kv_block[:, kv_width:].reshape(key_block, KVH, HD)
            scores, visible = block_scores(query_groups, keys_block, kpos, row_pos, score_scale)
            probs = jnp.where(visible, jnp.exp(scores - lse[..., None]), 0.0)
            d_probs = jnp.einsum(
                "hrd,khd->hrk", grad_groups, vals_block, preferred_element_type=jnp.float32
            )
            return (delta_now + jnp.sum(probs * d_probs, axis=-1), None)

        delta, _ = lax.scan(
            delta_step, jnp.zeros((KVH, row_count), jnp.float32), (kv_back, pos_blocks)
        )

        def grad_step(dq_now, item):
            kv_block, kpos = item
            keys_block = kv_block[:, :kv_width].reshape(key_block, KVH, HD)
            vals_block = kv_block[:, kv_width:].reshape(key_block, KVH, HD)
            scores, visible = block_scores(query_groups, keys_block, kpos, row_pos, score_scale)
            probs = jnp.where(visible, jnp.exp(scores - lse[..., None]), 0.0)
            d_probs = jnp.einsum(
                "hrd,khd->hrk", grad_groups, vals_block, preferred_element_type=jnp.float32
            )
            d_scores = (probs * (d_probs - delta[..., None])).astype(jnp.bfloat16)
            dq_new = dq_now + jnp.einsum(
                "hrk,khd->hrd", d_scores, keys_block, preferred_element_type=jnp.float32
            )
            d_keys = (
                jnp.einsum(
                    "hrk,hrd->khd", d_scores, query_groups, preferred_element_type=jnp.float32
                )
                * score_scale
            )
            d_vals = jnp.einsum(
                "hrk,hrd->khd",
                probs.astype(jnp.bfloat16),
                grad_groups,
                preferred_element_type=jnp.float32,
            )
            return (
                dq_new,
                jnp.concatenate(
                    [d_keys.reshape(key_block, kv_width), d_vals.reshape(key_block, kv_width)],
                    axis=1,
                ),
            )

        dq_groups, dkv_blocks = lax.scan(
            grad_step, jnp.zeros((KVH, row_count, HD), jnp.float32), (kv_back, pos_blocks)
        )
        dkv_mine = lax.psum_scatter(
            dkv_blocks.reshape(seq_len, 2 * kv_width), "ctx", scatter_dimension=0, tiled=True
        )
        d_query = (
            (dq_groups * score_scale)
            .reshape(KVH, group_size, seg_rows, HD)
            .transpose(2, 0, 1, 3)
            .reshape(seg_rows, QH, HD)
        )
        d_q_low = unrotate(d_query, cosine, sine).reshape(seg_rows, QH * HD).astype(jnp.bfloat16)
        d_key = unrotate(dkv_mine[:, :kv_width].reshape(seg_rows, KVH, HD), cosine, sine).reshape(
            seg_rows, kv_width
        )
        d_kv_low = jnp.concatenate([d_key, dkv_mine[:, kv_width:]], axis=1).astype(jnp.bfloat16)
        grad_q = outer_sum(act_one, d_q_low)
        grad_kv = outer_sum(act_one, d_kv_low)
        d_act_one = back_product(d_q_low, weight_q) + back_product(d_kv_low, weight_kv)
        d_in_norm, grad_gain_one = pull_one(d_act_one)
        input_grads.append((d_mid + d_in_norm).astype(jnp.bfloat16))
        parts_now = [grad_gain_one, grad_gain_two, grad_q, grad_kv, grad_o, grad_gu, grad_down]
        grad_names = [total + piece for total, piece in zip(grad_names, parts_now)]
    owned = (
        lax.psum_scatter(
            grad_names[0].astype(jnp.bfloat16), "wt", scatter_dimension=0, tiled=True
        ).astype(jnp.float32),
        lax.psum_scatter(
            grad_names[1].astype(jnp.bfloat16), "wt", scatter_dimension=0, tiled=True
        ).astype(jnp.float32),
        lax.psum_scatter(
            grad_names[2].astype(jnp.bfloat16), "wt", scatter_dimension=0, tiled=True
        ).astype(jnp.float32),
        lax.psum_scatter(
            grad_names[3].astype(jnp.bfloat16), "wt", scatter_dimension=0, tiled=True
        ).astype(jnp.float32),
        lax.psum_scatter(
            grad_names[4].astype(jnp.bfloat16), "wt", scatter_dimension=0, tiled=True
        ).astype(jnp.float32),
        lax.psum_scatter(
            grad_names[5].astype(jnp.bfloat16), "wt", scatter_dimension=0, tiled=True
        ).astype(jnp.float32),
        lax.psum_scatter(
            grad_names[6].astype(jnp.bfloat16), "wt", scatter_dimension=0, tiled=True
        ).astype(jnp.float32),
    )
    summed = lax.psum((owned[0], owned[1], owned[2], owned[3], owned[4], owned[5], owned[6]), "ctx")
    hidden_out = jnp.stack(outputs)[:, None]
    grad_in = jnp.stack(input_grads)[:, None]
    return (
        hidden_out,
        grad_in,
        summed[0],
        summed[1],
        summed[2],
        summed[3],
        summed[4],
        summed[5],
        summed[6],
    )


def solution(mesh):
    placed = (
        P(None, "wt", "ctx", None),
        P(None, "wt", "ctx", None),
        P(),
        P("wt"),
        P("wt"),
        P("wt", None),
        P("wt", None),
        P("wt", None),
        P("wt", None),
        P("wt", None),
    )
    return jax.shard_map(
        local,
        mesh=mesh,
        in_specs=placed,
        out_specs=(
            P(None, "wt", "ctx", None),
            P(None, "wt", "ctx", None),
            P("wt"),
            P("wt"),
            P("wt", None),
            P("wt", None),
            P("wt", None),
            P("wt", None),
            P("wt", None),
        ),
        check_vma=False,
    )
```

profile of v0, /device:TPU:0, one launch (start us, length us, event | category | flops | bytes accessed | tf_op | source)
XLA Modules:
  0.0 1084.1 jit_solution(5646645169143521290)
XLA Ops:
  12.4 8.3 all-reduce.6
  23.4 6.6 all-gather.10.cloned.1.call-done
  37.8 15.7 %all-gather.8.cloned.1.call-done = bf16[960,960]{1,0:T(8,128)(2,1)} async-done(((bf16[240,960]{1,0:T(8,128)(2,1)}), bf16[960,960]{1,0:T(8,128)(2,1)}) %all-gather.8.cloned.1.call-update) | async-done | bytes 1843216 | tf_op jit(solution)/shard_map/all_gather | solution.py:88
  59.6 38.7 %all-gather.20.cloned.1.call-done = bf16[1024,640]{1,0:T(8,128)(2,1)} async-done(((bf16[128,640]{1,0:T(8,128)(2,1)}), bf16[1024,640]{1,0:T(8,128)(2,1)}) %all-gather.20.cloned.1.call-update) | async-done | bytes 1310736 | tf_op jit(solution)/shard_map/all_gather | solution.py:144
  110.2 31.5 %all-gather.12.cloned.1.call-done = bf16[1024,640]{1,0:T(8,128)(2,1)} async-done(((bf16[128,640]{1,0:T(8,128)(2,1)}), bf16[1024,640]{1,0:T(8,128)(2,1)}) %all-gather.12.cloned.1.call-update) | async-done | bytes 1310736 | tf_op jit(solution)/shard_map/all_gather | solution.py:144
  152.6 11.0 %all-gather.14.cloned.1.call-done = bf16[960,960]{1,0:T(8,128)(2,1)} async-done(((bf16[240,960]{1,0:T(8,128)(2,1)}), bf16[960,960]{1,0:T(8,128)(2,1)}) %all-gather.14.cloned.1.call-update) | async-done | bytes 1843216 | tf_op jit(solution)/shard_map/all_gather | solution.py:90
  168.5 63.0 %all-gather.16.cloned.1.call-done = bf16[960,5120]{1,0:T(8,128)(2,1)} async-done(((bf16[240,5120]{1,0:T(8,128)(2,1)}), bf16[960,5120]{1,0:T(8,128)(2,1)}) %all-gather.16.cloned.1.call-update) | async-done | bytes 9830416 | tf_op jit(solution)/shard_map/all_gather | solution.py:91
  231.6 7.1 fusion.88
  241.8 29.9 %all-gather.18.cloned.1.call-done = bf16[2560,960]{0,1:T(8,128)(2,1)} async-done(((bf16[640,960]{0,1:T(8,128)(2,1)}), bf16[2560,960]{0,1:T(8,128)(2,1)}) %all-gather.18.cloned.1.call-update) | async-done | bytes 4915216 | tf_op jit(solution)/shard_map/all_gather | solution.py:92
  271.7 5.5 multiply_convert_fusion.3
  277.2 5.2 multiply_convert_fusion.5
  294.3 6.6 multiply_reduce_fusion
  317.3 6.8 multiply_reduce_fusion.1
  349.1 37.0 %reduce-scatter.12.cloned.1.call-done = f32[128,640]{0,1:T(8,128)} async-done(((f32[1024,640]{0,1:T(8,128)}), f32[128,640]{0,1:T(8,128)}) %reduce-scatter.12.cloned.1.call-update) | async-done | bytes 327696 | tf_op jit(solution)/shard_map/reduce_scatter | solution.py:271
  388.0 71.2 %reduce-scatter.10.cloned.1.call-done = f32[128,640]{0,1:T(8,128)} async-done(((f32[1024,640]{0,1:T(8,128)}), f32[128,640]{0,1:T(8,128)}) %reduce-scatter.10.cloned.1.call-update) | async-done | bytes 327696 | tf_op jit(solution)/shard_map/reduce_scatter | solution.py:271
  470.1 7.9 copy.86
  478.0 9.6 fusion.7
  487.6 11.8 %add_convert_fusion = bf16[960,5120]{1,0:T(8,128)(2,1)} fusion(f32[960,5120]{1,0:T(8,128)} %fusion.7, bf16[128,2560]{1,0:T(8,128)(2,1)} %copy-done.46, bf16[128,2560]{1,0:T(8,128)(2,1)} %copy-done.45, f32[128,960]{0,1:T(8,128)S(1)} %get-tuple-element.300, f32[128]{0:T(128)S(1)} %fusion.78, f32[960]{0:T(1024)S(1)} %convert_element_type.227), kind=kOutput, calls=%fused_computation | convolution fusion | flops 1271111680 | bytes 31297792 | tf_op jit(solution)/shard_map/dot_general | solution.py:64
  512.3 12.9 %reduce-scatter.18.cloned.1.call-done = bf16[240,960]{1,0:T(8,128)(2,1)} async-done(((bf16[960,960]{1,0:T(8,128)(2,1)}), bf16[240,960]{1,0:T(8,128)(2,1)}) %reduce-scatter.18.cloned.1.call-update) | async-done | bytes 460816 | tf_op jit(solution)/shard_map/reduce_scatter | solution.py:305
  529.2 5.7 all-reduce.5
  537.3 16.5 %reduce-scatter.16.cloned.1.call-done = bf16[240,640]{1,0:T(8,128)(2,1)} async-done(((bf16[960,640]{1,0:T(8,128)(2,1)}), bf16[240,640]{1,0:T(8,128)(2,1)}) %reduce-scatter.16.cloned.1.call-update) | async-done | bytes 307216 | tf_op jit(solution)/shard_map/reduce_scatter | solution.py:302
  553.8 54.1 %reduce-scatter.22.cloned.1.call-done = bf16[640,960]{1,0:T(8,128)(2,1)} async-done(((bf16[2560,960]{1,0:T(8,128)(2,1)}), bf16[640,960]{1,0:T(8,128)(2,1)}) %reduce-scatter.22.cloned.1.call-update) | async-done | bytes 1228816
  610.0 81.4 %reduce-scatter.20.cloned.1.call-done = bf16[240,5120]{1,0:T(8,128)(2,1)} async-done(((bf16[960,5120]{1,0:T(8,128)(2,1)}), bf16[240,5120]{1,0:T(8,128)(2,1)}) %reduce-scatter.20.cloned.1.call-update) | async-done | bytes 2457616 | tf_op jit(solution)/shard_map/reduce_scatter | solution.py:308
  691.4 385.8 %all-reduce.8 = (f32[240]{0:T(256)}, f32[240]{0:T(256)}, f32[240,960]{1,0:T(8,128)}, f32[240,640]{1,0:T(8,128)}, f32[240,960]{1,0:T(8,128)}, /*index=5*/f32[240,5120]{1,0:T(8,128)}, f32[640,960]{0,1:T(8,128)}) all-reduce(f32[240]{0:T(256)S(1)} %get-tuple-element.314, ...), channel_id=1, replica_groups=mesh['ctx'=8,'wt'=4] {'ctx'}, use_global_device_ids=true, to_apply=%region_19.20 | all-reduce | flops 2458080 | bytes 14749440 | tf_op jit(solution)/shard_map/psum | solution.py:315
  (307 shorter events, 137.2 us)
Async XLA Ops:
  7.2 22.9 %all-gather.10.cloned.1.call-start = ((), (), s32[]{:S(2)}) async-start(), calls=%async_computation.8 | async-start | bytes 1536000 | tf_op jit(solution)/shard_map/all_gather | solution.py:89
  7.9 45.6 %all-gather.8.cloned.1.call-start = ((), (), s32[]{:S(2)}) async-start(), calls=%async_computation.7 | async-start | bytes 2457600 | tf_op jit(solution)/shard_map/all_gather | solution.py:88
  8.7 89.7 %all-gather.20.cloned.1.call-start = ((), (), s32[]{:S(2)}) async-start(), calls=%async_computation.13 | async-start | bytes 1474560 | tf_op jit(solution)/shard_map/all_gather | solution.py:144
  23.4 34.7 %copy-start.49 = (f32[128,32]{0,1:T(8,128)}, f32[128,32]{0,1:T(8,128)S(1)}, u32[]{:S(2)}) copy-start(f32[128,32]{0,1:T(8,128)S(1)} %get-tuple-element.295) | copy-start | bytes 49156
  23.4 34.7 %copy-start.51 = (f32[128,32]{0,1:T(8,128)}, f32[128,32]{0,1:T(8,128)S(1)}, u32[]{:S(2)}) copy-start(f32[128,32]{0,1:T(8,128)S(1)} %get-tuple-element.296) | copy-start | bytes 49156
  33.3 108.4 %all-gather.12.cloned.1.call-start = ((), (), s32[]{:S(2)}) async-start(), calls=%async_computation.9 | async-start | bytes 1474560 | tf_op jit(solution)/shard_map/all_gather | solution.py:144
  35.2 128.5 %all-gather.14.cloned.1.call-start = ((), (), s32[]{:S(2)}) async-start(), calls=%async_computation.10 | async-start | bytes 2457600 | tf_op jit(solution)/shard_map/all_gather | solution.py:90
  35.8 195.8 %all-gather.16.cloned.1.call-start = ((), (), s32[]{:S(2)}) async-start(), calls=%async_computation.11 | async-start | bytes 12288000 | tf_op jit(solution)/shard_map/all_gather | solution.py:91
  36.4 235.3 %all-gather.18.cloned.1.call-start = ((), (), s32[]{:S(2)}) async-start(), calls=%async_computation.12 | async-start | bytes 6144000 | tf_op jit(solution)/shard_map/all_gather | solution.py:92
  37.1 349.0 %reduce-scatter.12.cloned.1.call-start = ((), (), s32[]{:S(2)}) async-start(), calls=%async_computation.15 | async-start | bytes 2949120 | tf_op jit(solution)/shard_map/reduce_scatter | solution.py:271
  37.5 70.0 %copy-start.12 = (pred[384,1024]{1,0:T(8,128)(4,1)}, pred[384,1024]{1,0:T(8,128)(4,1)S(1)}, u32[]{:S(2)}) copy-start(pred[384,1024]{1,0:T(8,128)(4,1)S(1)} %broadcast_compare_fusion) | copy-start | bytes 1179652
  37.8 112.5 %copy-start.10 = (pred[384,1024]{1,0:T(8,128)(4,1)}, pred[384,1024]{1,0:T(8,128)(4,1)S(1)}, u32[]{:S(2)}) copy-start(pred[384,1024]{1,0:T(8,128)(4,1)S(1)} %broadcast_compare_fusion.1) | copy-start | bytes 1179652
  59.0 46.1 %copy-start.37 = (bf16[5,384,64]{1,2,0:T(8,128)(2,1)}, bf16[5,384,64]{1,2,0:T(8,128)(2,1)S(1)}, u32[]{:S(2)}) copy-start(bf16[5,384,64]{1,2,0:T(8,128)(2,1)S(1)} %reshape.569) | copy-start | bytes 737284
  59.6 86.4 %copy-start.35 = (bf16[5,384,64]{1,2,0:T(8,128)(2,1)}, bf16[5,384,64]{1,2,0:T(8,128)(2,1)S(1)}, u32[]{:S(2)}) copy-start(bf16[5,384,64]{1,2,0:T(8,128)(2,1)S(1)} %reshape.564) | copy-start | bytes 737284
  110.2 53.5 %copy-start.29 = (bf16[128,5,3,64]{0,3,2,1:T(8,128)(2,1)}, bf16[128,5,3,64]{0,3,2,1:T(8,128)(2,1)S(1)}, u32[]{:S(2)}) copy-start(bf16[128,5,3,64]{0,3,2,1:T(8,128)(2,1)S(1)} %copy.79) | copy-start | bytes 737284
  152.6 86.0 %copy-start.31 = (bf16[128,5,3,64]{0,3,2,1:T(8,128)(2,1)}, bf16[128,5,3,64]{0,3,2,1:T(8,128)(2,1)S(1)}, u32[]{:S(2)}) copy-start(bf16[128,5,3,64]{0,3,2,1:T(8,128)(2,1)S(1)} %copy.72) | copy-start | bytes 737284
  238.7 33.0 %copy-start.26 = (bf16[2,1,128,960]{2,3,1,0:T(8,128)(2,1)S(1)}, bf16[2,1,128,960]{2,3,1,0:T(8,128)(2,1)}, u32[]{:S(2)}) copy-start(bf16[2,1,128,960]{2,3,1,0:T(8,128)(2,1)} %param.11) | copy-start | bytes 1474564
  315.0 144.2 %reduce-scatter.10.cloned.1.call-start = ((), (), s32[]{:S(2)}) async-start(), calls=%async_computation.14 | async-start | bytes 2949120 | tf_op jit(solution)/shard_map/reduce_scatter | solution.py:271
  333.4 178.9 %reduce-scatter.14.cloned.1.call-start = ((), (), s32[]{:S(2)}) async-start(), calls=%async_computation.16 | async-start | bytes 2457600 | tf_op jit(solution)/shard_map/reduce_scatter | solution.py:299
  346.0 179.3 %reduce-scatter.18.cloned.1.call-start = ((), (), s32[]{:S(2)}) async-start(), calls=%async_computation.18 | async-start | bytes 2457600 | tf_op jit(solution)/shard_map/reduce_scatter | solution.py:305
  349.1 204.7 %reduce-scatter.16.cloned.1.call-start = ((), (), s32[]{:S(2)}) async-start(), calls=%async_computation.17 | async-start | bytes 1536000 | tf_op jit(solution)/shard_map/reduce_scatter | solution.py:302
  387.1 76.4 %copy-start.42 = (bf16[128,320]{0,1:T(8,128)(2,1)}, bf16[128,320]{0,1:T(8,128)(2,1)S(1)}, u32[]{:S(2)}) copy-start(bf16[128,320]{0,1:T(8,128)(2,1)S(1)} %slice.310) | copy-start | bytes 245764
  463.5 144.4 %reduce-scatter.22.cloned.1.call-start = ((), (), s32[]{:S(2)}) async-start(), calls=%async_computation.20 | async-start | bytes 6553600
  478.0 213.4 %reduce-scatter.20.cloned.1.call-start = ((), (), s32[]{:S(2)}) async-start(), calls=%async_computation.19 | async-start | bytes 12288000 | tf_op jit(solution)/shard_map/reduce_scatter | solution.py:308
  (60 other events, 373.4 us)
Sparse Core Ops, SparseCore 0:
  9.6 20.4 all-gather.9
  31.6 21.8 all-gather.7
  56.3 42.0 all-gather.19
  101.0 40.6 all-gather.11
  143.1 20.5 all-gather.13
  165.1 66.4 all-gather.15
  233.1 38.5 all-gather.17
  315.1 70.9 reduce-scatter.11
  389.7 69.5 reduce-scatter.9
  462.2 29.5 reduce-scatter.13
  494.6 30.6 reduce-scatter.17
  527.7 26.0 reduce-scatter.15
  556.5 51.3 reduce-scatter.21
  610.4 80.9 reduce-scatter.19
where the time goes:
time: 1090 us; the launch traced here: 1080 us
  waiting for transfers between devices  473 us (43%)
  blocking collectives  400 us (37%)
  matrix products  126 us (12%)
  local copies, waits for them, and re-layouts  40.6 us (4%)
  other arithmetic  27.4 us (3%)
  between operations  17 us (2%)
    psum x1, blocking collectives, local(): lax.psum((owned[0], owned[1], owned[2], owned[3], owned[4], owned[5], own...  386 us
    reduce_scatter x2, waiting for transfers between devices, local(): lax.psum_scatter(dkv_blocks.reshape(seq_len, 2 * kv_width), 'ctx', scatte...  108 us
    reduce_scatter x1, waiting for transfers between devices, local(): lax.psum_scatter(grad_names[5].astype(jnp.bfloat16), 'wt', scatter_dimens...  81.4 us
    all_gather x2, waiting for transfers between devices, local(): kv_whole = lax.all_gather(kv_send, 'ctx', axis=0, tiled=True)  70.2 us
    all_gather x1, waiting for transfers between devices, local(): lax.all_gather(w_gu, 'wt', axis=0, tiled=True)  63 us
    unnamed x15, waiting for transfers between devices  57.4 us
    dot_general x10, matrix products, outer_sum(): lax.dot_general(left, right, (((0,), (0,)), ((), ())), preferred_element_...  35.2 us
    all_gather x1, waiting for transfers between devices, local(): lax.all_gather(w_down, 'wt', axis=0, tiled=True)  29.9 us
  transfers between devices with their start and end apart: 14, of which 13 were waited for; matrix products, arithmetic and copies ran while one was open for 14% of the time, Pallas kernels for 0%

commit v1 on v0

--- a/solution.py
+++ b/solution.py
@@ -141,7 +141,14 @@
             seg_rows, kv_width
         )
         kv_send = jnp.concatenate([key_rot, kv_lin[:, kv_width:]], axis=1).astype(jnp.bfloat16)
-        kv_whole = lax.all_gather(kv_send, "ctx", axis=0, tiled=True)
+        ring = [kv_send]
+        for hop in range(7):
+            ring.append(lax.ppermute(ring[-1], "ctx", [(dev, (dev + 1) % 8) for dev in range(8)]))
+        kv_whole = jnp.roll(
+            jnp.concatenate(ring[::-1], axis=0),
+            (lax.axis_index("ctx") + 1) * ring[0].shape[0],
+            axis=0,
+        )
         kv_blocks = kv_whole.reshape(block_count, key_block, 2 * kv_width)
         pos_blocks = key_pos.reshape(block_count, key_block)
 

time: 1090 us -> 1050 us (0.963)
  waiting for transfers between devices: 473 us -> 401 us
  local copies, waits for them, and re-layouts: 40.6 us -> 65 us
    all_gather x2, waiting for transfers between devices: 70.2 us -> 6.55 us  [local(): lax.all_gather(kv_send, 'ctx', axis=0, tiled=True)]
    ppermute x0 -> x14, waiting for transfers between devices: none -> 55.5 us  [local(): lax.ppermute(ring[-1], 'ctx', [(dev, (dev + 1) % 8) for dev in range(8)])]
    all_gather x1, waiting for transfers between devices: 63 us -> 36.6 us  [local(): lax.all_gather(w_gu, 'wt', axis=0, tiled=True)]
    all_gather x1, waiting for transfers between devices: 15.7 us -> 0.01 us  [local(): lax.all_gather(w_q, 'wt', axis=0, tiled=True)]
    slice x0 -> x6, local copies, waits for them, and re-layouts: none -> 14.7 us  [the longest x4 10.3 us: grad_step(): keys_block = kv_block[:, :kv_width].reshape(key_block, KVH, HD)]
    unnamed x147 -> x231, local copies, waits for them, and re-layouts: 17.7 us -> 30.5 us
    dot_general x2 -> x4, matrix products: 3.13 us -> 14.4 us  [block_scores(): jnp.einsum('hrd,khd->hrk', query_groups, keys_block, preferred_element_ty...]
    all_gather x1, waiting for transfers between devices: 11 us -> 0.02 us  [local(): lax.all_gather(w_o, 'wt', axis=0, tiled=True)]
  transfers between devices with their start and end apart: 14 -> 28, of which waited for: 13 -> 22; matrix products, arithmetic and copies ran while one was open for 14% -> 21% of each run, Pallas kernels for 0% -> 0%
where the time goes in v1:
time: 1050 us
  waiting for transfers between devices  401 us (38%)
  blocking collectives  400 us (38%)
  matrix products  132 us (13%)
  local copies, waits for them, and re-layouts  65 us (6%)
  other arithmetic  26.6 us (3%)
  between operations  17.3 us (2%)
    psum x1, blocking collectives, local(): lax.psum((owned[0], owned[1], owned[2], owned[3], owned[4], owned[5], own...  386 us
    reduce_scatter x2, waiting for transfers between devices, local(): lax.psum_scatter(dkv_blocks.reshape(seq_len, 2 * kv_width), 'ctx', scatte...  98.9 us
    reduce_scatter x1, waiting for transfers between devices, local(): lax.psum_scatter(grad_names[5].astype(jnp.bfloat16), 'wt', scatter_dimens...  81.4 us
    unnamed x15, waiting for transfers between devices  57.4 us
    ppermute x14, waiting for transfers between devices, local(): lax.ppermute(ring[-1], 'ctx', [(dev, (dev + 1) % 8) for dev in range(8)])  55.5 us
    all_gather x1, waiting for transfers between devices, local(): lax.all_gather(w_gu, 'wt', axis=0, tiled=True)  36.6 us
    dot_general x10, matrix products, outer_sum(): lax.dot_general(left, right, (((0,), (0,)), ((), ())), preferred_element_...  35.1 us
    unnamed x231, local copies, waits for them, and re-layouts  30.5 us
  transfers between devices with their start and end apart: 28, of which 22 were waited for; matrix products, arithmetic and copies ran while one was open for 21% of the time, Pallas kernels for 0%

profile of v1, /device:TPU:0, one launch (start us, length us, event | category | flops | bytes accessed | tf_op | source)
XLA Modules:
  0.0 1046.6 jit_solution(13362910513926880227)
XLA Ops:
  13.1 8.3 all-reduce.6
  24.2 5.9 all-gather.10.cloned.1.call-done
  38.7 5.6 collective-permute-done.7
  47.2 5.6 collective-permute-done.8
  94.8 6.8 collective-permute-done.13
  146.5 5.6 fusion.119
  154.3 36.6 %all-gather.14.cloned.1.call-done = bf16[960,5120]{1,0:T(8,128)(2,1)} async-done(((bf16[240,5120]{1,0:T(8,128)(2,1)}), bf16[960,5120]{1,0:T(8,128)(2,1)}) %all-gather.14.cloned.1.call-update) | async-done | bytes 9830416 | tf_op jit(solution)/shard_map/all_gather | solution.py:91
  190.9 7.1 fusion.110
  201.4 29.5 %all-gather.16.cloned.1.call-done = bf16[2560,960]{0,1:T(8,128)(2,1)} async-done(((bf16[640,960]{0,1:T(8,128)(2,1)}), bf16[2560,960]{0,1:T(8,128)(2,1)}) %all-gather.16.cloned.1.call-update) | async-done | bytes 4915216 | tf_op jit(solution)/shard_map/all_gather | solution.py:92
  253.6 6.6 multiply_reduce_fusion
  268.7 6.5 all-gather.18.cloned.1.call-done
  282.6 5.7 fusion.118
  289.4 7.0 multiply_reduce_fusion.1
  321.2 27.3 %reduce-scatter.12.cloned.1.call-done = f32[128,640]{0,1:T(8,128)} async-done(((f32[1024,640]{0,1:T(8,128)}), f32[128,640]{0,1:T(8,128)}) %reduce-scatter.12.cloned.1.call-update) | async-done | bytes 327696 | tf_op jit(solution)/shard_map/reduce_scatter | solution.py:278
  350.3 71.6 %reduce-scatter.10.cloned.1.call-done = f32[128,640]{0,1:T(8,128)} async-done(((f32[1024,640]{0,1:T(8,128)}), f32[128,640]{0,1:T(8,128)}) %reduce-scatter.10.cloned.1.call-update) | async-done | bytes 327696 | tf_op jit(solution)/shard_map/reduce_scatter | solution.py:278
  432.5 7.9 copy.96
  440.7 9.6 fusion.21
  450.3 11.8 %add_convert_fusion = bf16[960,5120]{1,0:T(8,128)(2,1)} fusion(f32[960,5120]{1,0:T(8,128)} %fusion.21, bf16[128,2560]{1,0:T(8,128)(2,1)} %copy-done.42, bf16[128,2560]{1,0:T(8,128)(2,1)} %copy-done.41, f32[128,960]{0,1:T(8,128)S(1)} %get-tuple-element.305, f32[128]{0:T(128)S(1)} %fusion.92, f32[960]{0:T(1024)S(1)} %convert_element_type.231), kind=kOutput, calls=%fused_computation | convolution fusion | flops 1271111680 | bytes 31297792 | tf_op jit(solution)/shard_map/dot_general | solution.py:64
  474.9 13.0 %reduce-scatter.18.cloned.1.call-done = bf16[240,960]{1,0:T(8,128)(2,1)} async-done(((bf16[960,960]{1,0:T(8,128)(2,1)}), bf16[240,960]{1,0:T(8,128)(2,1)}) %reduce-scatter.18.cloned.1.call-update) | async-done | bytes 460816 | tf_op jit(solution)/shard_map/reduce_scatter | solution.py:312
  491.8 5.7 all-reduce.5
  499.9 16.5 %reduce-scatter.16.cloned.1.call-done = bf16[240,640]{1,0:T(8,128)(2,1)} async-done(((bf16[960,640]{1,0:T(8,128)(2,1)}), bf16[240,640]{1,0:T(8,128)(2,1)}) %reduce-scatter.16.cloned.1.call-update) | async-done | bytes 307216 | tf_op jit(solution)/shard_map/reduce_scatter | solution.py:309
  516.4 54.2 %reduce-scatter.22.cloned.1.call-done = bf16[640,960]{1,0:T(8,128)(2,1)} async-done(((bf16[2560,960]{1,0:T(8,128)(2,1)}), bf16[640,960]{1,0:T(8,128)(2,1)}) %reduce-scatter.22.cloned.1.call-update) | async-done | bytes 1228816
  572.7 81.4 %reduce-scatter.20.cloned.1.call-done = bf16[240,5120]{1,0:T(8,128)(2,1)} async-done(((bf16[960,5120]{1,0:T(8,128)(2,1)}), bf16[240,5120]{1,0:T(8,128)(2,1)}) %reduce-scatter.20.cloned.1.call-update) | async-done | bytes 2457616 | tf_op jit(solution)/shard_map/reduce_scatter | solution.py:315
  654.1 385.7 %all-reduce.8 = (f32[240]{0:T(256)}, f32[240]{0:T(256)}, f32[240,960]{1,0:T(8,128)}, f32[240,640]{1,0:T(8,128)}, f32[240,960]{1,0:T(8,128)}, /*index=5*/f32[240,5120]{1,0:T(8,128)}, f32[640,960]{0,1:T(8,128)}) all-reduce(f32[240]{0:T(256)S(1)} %get-tuple-element.319, ...), channel_id=1, replica_groups=mesh['ctx'=8,'wt'=4] {'ctx'}, use_global_device_ids=true, to_apply=%region_19.21 | all-reduce | flops 2458080 | bytes 14749440 | tf_op jit(solution)/shard_map/psum | solution.py:322
  (432 shorter events, 207.7 us)
Async XLA Ops:
  7.2 22.9 %all-gather.10.cloned.1.call-start = ((), (), s32[]{:S(2)}) async-start(), calls=%async_computation.8 | async-start | bytes 1536000 | tf_op jit(solution)/shard_map/all_gather | solution.py:89
  7.9 75.8 %all-gather.8.cloned.1.call-start = ((), (), s32[]{:S(2)}) async-start(), calls=%async_computation.7 | async-start | bytes 2457600 | tf_op jit(solution)/shard_map/all_gather | solution.py:88
  8.7 111.3 %all-gather.12.cloned.1.call-start = ((), (), s32[]{:S(2)}) async-start(), calls=%async_computation.9 | async-start | bytes 2457600 | tf_op jit(solution)/shard_map/all_gather | solution.py:90
  9.4 132.0 %all-gather.20.cloned.1.call-start = ((), (), s32[]{:S(2)}) async-start(), calls=%async_computation.14 | async-start | bytes 1474560 | tf_op jit(solution)/shard_map/all_gather | solution.py:223
  33.3 157.7 %all-gather.14.cloned.1.call-start = ((), (), s32[]{:S(2)}) async-start(), calls=%async_computation.10 | async-start | bytes 12288000 | tf_op jit(solution)/shard_map/all_gather | solution.py:91
  33.9 197.0 %all-gather.16.cloned.1.call-start = ((), (), s32[]{:S(2)}) async-start(), calls=%async_computation.11 | async-start | bytes 6144000 | tf_op jit(solution)/shard_map/all_gather | solution.py:92
  34.5 240.7 %all-gather.18.cloned.1.call-start = ((), (), s32[]{:S(2)}) async-start(), calls=%async_computation.12 | async-start | bytes 1474560 | tf_op jit(solution)/shard_map/all_gather | solution.py:223
  34.5 9.8 collective-permute-start.7
  37.2 10.0 collective-permute-start
  47.1 9.3 collective-permute-start.1
  56.4 9.7 collective-permute-start.2
  61.5 9.7 collective-permute-start.10
  66.2 8.9 collective-permute-start.3
  71.2 9.2 collective-permute-start.11
  75.5 273.0 %reduce-scatter.12.cloned.1.call-start = ((), (), s32[]{:S(2)}) async-start(), calls=%async_computation.15 | async-start | bytes 2949120 | tf_op jit(solution)/shard_map/reduce_scatter | solution.py:278
  83.7 10.6 %collective-permute-start.5 = (bf16[128,640]{1,0:T(8,128)(2,1)}, bf16[128,640]{1,0:T(8,128)(2,1)}, u32[]{:S(2)}, u32[]{:S(2)}) collective-permute-start(bf16[128,640]{1,0:T(8,128)(2,1)} %collective-permute-done.4), channel_id=1, source_target_pairs={{0,4},{4,8},{8,12},{12,16},{16,20},{20,24},{24,28},{28,0},{1,5},{5... | collective-permute-start | bytes 491528 | tf_op jit(solution)/shard_map/ppermute | solution.py:146
  88.7 12.9 %collective-permute-start.13 = (bf16[128,640]{1,0:T(8,128)(2,1)}, bf16[128,640]{1,0:T(8,128)(2,1)}, u32[]{:S(2)}, u32[]{:S(2)}) collective-permute-start(bf16[128,640]{1,0:T(8,128)(2,1)} %collective-permute-done.12), channel_id=1, source_target_pairs={{0,4},{4,8},{8,12},{12,16},{16,20},{20,24},{24,28},{28,0},{1,5},{5... | collective-permute-start | bytes 491528 | tf_op jit(solution)/shard_map/ppermute | solution.py:146
  94.3 28.2 %collective-permute-start.6 = (bf16[128,640]{1,0:T(8,128)(2,1)}, bf16[128,640]{1,0:T(8,128)(2,1)}, u32[]{:S(2)}, u32[]{:S(2)}) collective-permute-start(bf16[128,640]{1,0:T(8,128)(2,1)} %collective-permute-done.5), channel_id=1, source_target_pairs={{0,4},{4,8},{8,12},{12,16},{16,20},{20,24},{24,28},{28,0},{1,5},{5... | collective-permute-start | bytes 491528 | tf_op jit(solution)/shard_map/ppermute | solution.py:146
  268.6 153.3 %reduce-scatter.10.cloned.1.call-start = ((), (), s32[]{:S(2)}) async-start(), calls=%async_computation.13 | async-start | bytes 2949120 | tf_op jit(solution)/shard_map/reduce_scatter | solution.py:278
  304.5 170.4 %reduce-scatter.14.cloned.1.call-start = ((), (), s32[]{:S(2)}) async-start(), calls=%async_computation.16 | async-start | bytes 2457600 | tf_op jit(solution)/shard_map/reduce_scatter | solution.py:306
  318.1 169.9 %reduce-scatter.18.cloned.1.call-start = ((), (), s32[]{:S(2)}) async-start(), calls=%async_computation.18 | async-start | bytes 2457600 | tf_op jit(solution)/shard_map/reduce_scatter | solution.py:312
  321.1 195.3 %reduce-scatter.16.cloned.1.call-start = ((), (), s32[]{:S(2)}) async-start(), calls=%async_computation.17 | async-start | bytes 1536000 | tf_op jit(solution)/shard_map/reduce_scatter | solution.py:309
  426.2 144.4 %reduce-scatter.22.cloned.1.call-start = ((), (), s32[]{:S(2)}) async-start(), calls=%async_computation.20 | async-start | bytes 6553600
  440.5 213.6 %reduce-scatter.20.cloned.1.call-start = ((), (), s32[]{:S(2)}) async-start(), calls=%async_computation.19 | async-start | bytes 12288000 | tf_op jit(solution)/shard_map/reduce_scatter | solution.py:315
  (109 other events, 1967.8 us)
Sparse Core Ops, SparseCore 0:
  9.6 20.4 all-gather.9
  31.6 21.8 all-gather.7
  55.1 21.8 all-gather.11
  79.6 44.5 all-gather.19
  125.6 65.3 all-gather.13
  192.4 38.5 all-gather.15
  233.1 42.0 all-gather.17
  278.7 69.7 reduce-scatter.11
  352.0 69.8 reduce-scatter.9
  424.9 29.5 reduce-scatter.13
  457.2 30.6 reduce-scatter.17
  490.4 26.0 reduce-scatter.15
  519.1 51.4 reduce-scatter.21
  573.1 80.9 reduce-scatter.19
